TPU v7x, 32 devices: a whole 2x2x4 slice. The times are simulated.
32 devices in a mesh: fsdp: 4 (over x, core), ctx: 2 (over y), tp: 4 (over z).
Axes of the slice: x: 2, y: 2, z: 4, core: 2. Of those that a mesh axis runs over, the one named last changes fastest.
Arguments:
- tokens: bfloat16 [8, 1024, 2048], P('fsdp', 'ctx'), may hold values from -6 to 6
- attn_gain: bfloat16 [2048], P('fsdp'), may hold values from 0.5 to 1.5
- w_query: bfloat16 [2048, 1024], P('fsdp', 'tp'), may hold values from -0.125 to 0.125
- key_matrix: bfloat16 [2048, 256], P('fsdp', 'tp'), may hold values from -0.125 to 0.125
- value_matrix: bfloat16 [2048, 256], P('fsdp', 'tp'), may hold values from -0.125 to 0.125
- query_gain: bfloat16 [64], P('fsdp'), may hold values from 0.5 to 1.5
- key_gain: bfloat16 [64], P('fsdp'), may hold values from 0.5 to 1.5
- w_out: bfloat16 [1024, 2048], P('tp', 'fsdp'), may hold values from -6 to 6
- ffn_gain: bfloat16 [2048], P('fsdp'), may hold values from 0.5 to 1.5
- w_gate: bfloat16 [2048, 1024], P('fsdp', 'tp'), may hold values from -0.125 to 0.125
- w_up: bfloat16 [2048, 1024], P('fsdp', 'tp'), may hold values from -0.125 to 0.125
- w_down: bfloat16 [1024, 2048], P('tp', 'fsdp'), may hold values from -0.1875 to 0.1875
- prefix_len: int32 [8], P('fsdp'), may hold values from 102 to 512
- out_grad: bfloat16 [8, 1024, 2048], P('fsdp', 'ctx'), may hold values from -6 to 6
Outputs:
- layer_out: bfloat16 [8, 1024, 2048], P('fsdp', 'ctx')
- input_grad: bfloat16 [8, 1024, 2048], P('fsdp', 'ctx')
- grad_attn_gain: float32 [2048], P('fsdp')
- grad_query: float32 [2048, 1024], P('fsdp', 'tp')
- grad_key: float32 [2048, 256], P('fsdp', 'tp')
- grad_value: float32 [2048, 256], P('fsdp', 'tp')
- grad_query_gain: float32 [64], P('fsdp')
- grad_key_gain: float32 [64], P('fsdp')
- grad_out: float32 [1024, 2048], P('tp', 'fsdp')
- grad_ffn_gain: float32 [2048], P('fsdp')
- grad_gate: float32 [2048, 1024], P('fsdp', 'tp')
- grad_up: float32 [2048, 1024], P('fsdp', 'tp')
- grad_down: float32 [1024, 2048], P('tp', 'fsdp')
All inputs are finite; a program needn't handle non-finite values.
Results may differ from a plain program's by a relative error of at most 0.025.
Values may be sent and summed in bfloat16 or wider, within the bound.
No kernel may reach another device: no remote copies, remote signals or barrier semaphores. Data moves between devices by JAX's collectives and lax.ppermute only.
A program may use at most 192 MiB of HBM per device.

v0:
```python
import functools
import jax
import jax.numpy as jnp
from jax import lax
from jax.sharding import PartitionSpec as P

EPSILON = 1e-06
NEGATIVE = -1e30
ROPE_BASE = 10000.0


def rms_norm(values, gain):
    return values * lax.rsqrt(jnp.mean(values * values, axis=-1, keepdims=True) + EPSILON) * gain


def rotate(values, cos_table, sin_table):
    half_dim = values.shape[-1] // 2
    turned = jnp.concatenate([-values[..., half_dim:], values[..., :half_dim]], axis=-1)
    return values * cos_table + turned * sin_table


def rotary_tables(positions, head_dim):
    inverse_freq = ROPE_BASE ** (-jnp.arange(0, head_dim, 2).astype(jnp.float32) / head_dim)
    angles = positions.astype(jnp.float32)[:, None] * inverse_freq[None, :]
    cos_half = jnp.cos(angles)
    sin_half = jnp.sin(angles)
    return (jnp.concatenate([cos_half, cos_half], -1), jnp.concatenate([sin_half, sin_half], -1))


def query_key_post(
    query_raw, unnormed_key, query_gain, key_gain, cos_table, sin_table, seq_count, block_len
):
    head_dim = query_gain.shape[0]
    query_heads = query_raw.reshape(seq_count, block_len, -1, head_dim)
    key_heads = unnormed_key.reshape(seq_count, block_len, -1, head_dim)
    cos_wide = cos_table[None, :, None, :]
    sin_wide = sin_table[None, :, None, :]
    return (
        rotate(rms_norm(query_heads, query_gain), cos_wide, sin_wide),
        rotate(rms_norm(key_heads, key_gain), cos_wide, sin_wide),
    )


def swiglu(gate_proj, up_proj):
    return jax.nn.silu(gate_proj) * up_proj


def outer_sum(left, right):
    return lax.dot_general(
        left, right, (((0,), (0,)), ((), ())), preferred_element_type=jnp.float32
    )


def times_transposed(left, right):
    return lax.dot_general(
        left, right, (((1,), (1,)), ((), ())), preferred_element_type=jnp.float32
    )


def pack_grads(gradients, grad_dims, pieces):
    columns = [
        jnp.moveaxis(gradient, dim_index, 0).reshape(pieces, -1)
        for gradient, dim_index in zip(gradients, grad_dims)
    ]
    return jnp.concatenate(columns, axis=1)


def unpack_grads(packed, gradients, grad_dims, pieces):
    results = []
    offset = 0
    for gradient, dim_index in zip(gradients, grad_dims):
        moved_shape = jnp.moveaxis(gradient, dim_index, 0).shape
        width = gradient.size // pieces
        segment = packed[:, offset : offset + width]
        offset = offset + width
        shaped = segment.reshape((-1,) + tuple(moved_shape[1:]))
        results.append(jnp.moveaxis(shaped, 0, dim_index))
    return results


def shards(
    tokens,
    attn_gain,
    w_query,
    key_matrix,
    value_matrix,
    query_gain,
    key_gain,
    w_out,
    ffn_gain,
    w_gate,
    w_up,
    w_down,
    prefix_len,
    out_grad,
):
    (
        full_attn_gain,
        full_query,
        full_key,
        full_value,
        full_query_gain,
        full_key_gain,
        full_out,
        full_ffn_gain,
        full_gate,
        full_up,
        full_down,
    ) = (
        lax.all_gather(attn_gain, "fsdp", axis=0, tiled=True),
        lax.all_gather(w_query, "fsdp", axis=0, tiled=True),
        lax.all_gather(key_matrix, "fsdp", axis=0, tiled=True),
        lax.all_gather(value_matrix, "fsdp", axis=0, tiled=True),
        lax.all_gather(query_gain, "fsdp", axis=0, tiled=True),
        lax.all_gather(key_gain, "fsdp", axis=0, tiled=True),
        lax.all_gather(w_out, "fsdp", axis=1, tiled=True),
        lax.all_gather(ffn_gain, "fsdp", axis=0, tiled=True),
        lax.all_gather(w_gate, "fsdp", axis=0, tiled=True),
        lax.all_gather(w_up, "fsdp", axis=0, tiled=True),
        lax.all_gather(w_down, "fsdp", axis=1, tiled=True),
    )
    seq_count, block_len, model_dim = tokens.shape
    token_rows = seq_count * block_len
    head_dim = full_query_gain.shape[0]
    head_count = full_query.shape[1] // head_dim
    kv_count = full_key.shape[1] // head_dim
    group_size = head_count // kv_count
    ctx_count = lax.axis_size("ctx")
    ctx_index = lax.axis_index("ctx")
    fsdp_count = lax.axis_size("fsdp")
    seq_len = block_len * ctx_count
    scale_factor = head_dim ** (-0.5)
    tp_count = lax.axis_size("tp")
    share_rows = token_rows // tp_count
    share_start = lax.axis_index("tp") * share_rows

    def own_rows(values):
        return lax.dynamic_slice_in_dim(values, share_start, share_rows, 0)

    query_pos = ctx_index * block_len + jnp.arange(block_len, dtype=jnp.int32)
    cos_table, sin_table = rotary_tables(query_pos, head_dim)
    attn_gain32 = full_attn_gain.astype(jnp.float32)
    ffn_gain32 = full_ffn_gain.astype(jnp.float32)
    query_gain32 = full_query_gain.astype(jnp.float32)
    key_gain32 = full_key_gain.astype(jnp.float32)
    inputs = tokens.astype(jnp.float32).reshape(token_rows, model_dim)
    normalized_input = rms_norm(inputs, attn_gain32).astype(jnp.bfloat16)
    query_raw = jnp.dot(normalized_input, full_query, preferred_element_type=jnp.float32)
    unnormed_key = jnp.dot(normalized_input, full_key, preferred_element_type=jnp.float32)
    value_reduced = jnp.dot(
        normalized_input, full_value, preferred_element_type=jnp.float32
    ).astype(jnp.bfloat16)
    post_fn = functools.partial(
        query_key_post,
        cos_table=cos_table,
        sin_table=sin_table,
        seq_count=seq_count,
        block_len=block_len,
    )
    (rotated_query, key_rot), post_pull = jax.vjp(
        post_fn, query_raw, unnormed_key, query_gain32, key_gain32
    )
    query_grp = rotated_query.astype(jnp.bfloat16).reshape(
        seq_count, block_len, kv_count, group_size, head_dim
    )
    key_low = key_rot.astype(jnp.bfloat16)
    value_heads = value_reduced.reshape(seq_count, block_len, kv_count, head_dim)
    keys_all, values_all = (
        lax.all_gather(key_low, "ctx", axis=1, tiled=True),
        lax.all_gather(value_heads, "ctx", axis=1, tiled=True),
    )
    key_blocks = jnp.moveaxis(
        keys_all.reshape(seq_count, ctx_count, block_len, kv_count, head_dim), 1, 0
    )
    value_blocks = jnp.moveaxis(
        values_all.reshape(seq_count, ctx_count, block_len, kv_count, head_dim), 1, 0
    )
    block_ids = jnp.arange(ctx_count, dtype=jnp.int32)

    def score_block(key_blk, block_id):
        raw_scores = (
            jnp.einsum("sqkgd,sjkd->skgqj", query_grp, key_blk, preferred_element_type=jnp.float32)
            * scale_factor
        )
        key_pos = block_id * block_len + jnp.arange(block_len, dtype=jnp.int32)
        causal = key_pos[None, :] <= query_pos[:, None]
        opened = key_pos[None, None, :] < prefix_len[:, None, None]
        allowed = causal[None] | opened
        return jnp.where(allowed[:, None, None], raw_scores, NEGATIVE)

    def max_step(run_state, scan_item):
        key_blk, block_id = scan_item
        run_max, run_sum = run_state
        scores = score_block(key_blk, block_id)
        new_max = jnp.maximum(run_max, jnp.max(scores, axis=-1))
        new_sum = run_sum * jnp.exp(run_max - new_max) + jnp.sum(
            jnp.exp(scores - new_max[..., None]), axis=-1
        )
        new_state = (new_max, new_sum)
        return (new_state, None)

    stat_shape = (seq_count, kv_count, group_size, block_len)
    (run_max, run_sum), _ = lax.scan(
        max_step,
        (jnp.full(stat_shape, NEGATIVE, jnp.float32), jnp.zeros(stat_shape, jnp.float32)),
        (key_blocks, block_ids),
    )
    log_total = run_max + jnp.log(run_sum)

    def out_step(running, scan_item):
        key_blk, value_blk, block_id = scan_item
        prob_vals = jnp.exp(score_block(key_blk, block_id) - log_total[..., None])
        new_running = running + jnp.einsum(
            "skgqj,sjkd->sqkgd",
            prob_vals.astype(jnp.bfloat16),
            value_blk,
            preferred_element_type=jnp.float32,
        )
        return (new_running, None)

    out_shape = (seq_count, block_len, kv_count, group_size, head_dim)
    attended, _ = lax.scan(
        out_step, jnp.zeros(out_shape, jnp.float32), (key_blocks, value_blocks, block_ids)
    )
    attended_low = attended.reshape(token_rows, head_count * head_dim).astype(jnp.bfloat16)
    attn_part = jnp.dot(attended_low, full_out, preferred_element_type=jnp.float32)
    residual = inputs + lax.psum(attn_part.astype(jnp.bfloat16), "tp").astype(jnp.float32)
    residual_own = own_rows(residual)
    ffn_in = rms_norm(residual, ffn_gain32).astype(jnp.bfloat16)
    gate_proj = jnp.dot(ffn_in, full_gate, preferred_element_type=jnp.float32)
    up_proj = jnp.dot(ffn_in, full_up, preferred_element_type=jnp.float32)
    hidden_f, swiglu_pull = jax.vjp(swiglu, gate_proj, up_proj)
    hidden = hidden_f.astype(jnp.bfloat16)
    ffn_part = jnp.dot(hidden, full_down, preferred_element_type=jnp.float32)
    layer_low = (
        residual + lax.psum(ffn_part.astype(jnp.bfloat16), "tp").astype(jnp.float32)
    ).astype(jnp.bfloat16)
    grad_low = out_grad.reshape(token_rows, model_dim)
    grad_down = outer_sum(hidden, grad_low)
    dhidden = times_transposed(grad_low, full_down)
    dgate_f, dup_f = swiglu_pull(dhidden)
    dgate = dgate_f.astype(jnp.bfloat16)
    dup = dup_f.astype(jnp.bfloat16)
    grad_gate = outer_sum(ffn_in, dgate)
    grad_up = outer_sum(ffn_in, dup)
    dffn_part = times_transposed(dgate, full_gate) + times_transposed(dup, full_up)
    dffn_in = lax.psum(dffn_part.astype(jnp.bfloat16), "tp").astype(jnp.float32)
    _, ffn_norm_pull = jax.vjp(rms_norm, residual, ffn_gain32)
    dres_norm, _ = ffn_norm_pull(dffn_in)
    dresidual = grad_low.astype(jnp.float32) + dres_norm
    _, own_pull = jax.vjp(rms_norm, residual_own, ffn_gain32)
    _, grad_ffn_gain = own_pull(own_rows(dffn_in))
    dres_low = dresidual.astype(jnp.bfloat16)
    grad_out = outer_sum(attended_low, dres_low)
    dattended = times_transposed(dres_low, full_out).astype(jnp.bfloat16)
    dout_grp = dattended.reshape(out_shape)
    delta = jnp.transpose(jnp.sum(dout_grp.astype(jnp.float32) * attended, axis=-1), (0, 2, 3, 1))

    def back_step(running, scan_item):
        key_blk, value_blk, block_id = scan_item
        prob_vals = jnp.exp(score_block(key_blk, block_id) - log_total[..., None])
        prob_low = prob_vals.astype(jnp.bfloat16)
        value_grad = jnp.einsum(
            "skgqj,sqkgd->sjkd", prob_low, dout_grp, preferred_element_type=jnp.float32
        )
        dprob = jnp.einsum(
            "sqkgd,sjkd->skgqj", dout_grp, value_blk, preferred_element_type=jnp.float32
        )
        dscore = (prob_vals * (dprob - delta[..., None])).astype(jnp.bfloat16)
        new_running = (
            running
            + jnp.einsum("skgqj,sjkd->sqkgd", dscore, key_blk, preferred_element_type=jnp.float32)
            * scale_factor
        )
        key_grad = (
            jnp.einsum("skgqj,sqkgd->sjkd", dscore, query_grp, preferred_element_type=jnp.float32)
            * scale_factor
        )
        return (new_running, (key_grad, value_grad))

    dquery_rot, (key_grads, value_grads) = lax.scan(
        back_step, jnp.zeros(out_shape, jnp.float32), (key_blocks, value_blocks, block_ids)
    )
    key_grads = jnp.moveaxis(key_grads, 0, 1).reshape(seq_count, seq_len, kv_count, head_dim)
    value_grads = jnp.moveaxis(value_grads, 0, 1).reshape(seq_count, seq_len, kv_count, head_dim)
    stacked_grads = jnp.stack((key_grads, value_grads), axis=0)
    owned_grads = lax.psum_scatter(
        stacked_grads.astype(jnp.bfloat16), "ctx", scatter_dimension=2, tiled=True
    ).astype(jnp.float32)
    dkey_rot = owned_grads[0]
    dvalue = owned_grads[1]
    dquery_raw, dkey_raw, grad_query_gain, grad_key_gain = post_pull(
        (dquery_rot.reshape(seq_count, block_len, head_count, head_dim), dkey_rot)
    )
    dq_low = dquery_raw.astype(jnp.bfloat16)
    dk_low = dkey_raw.astype(jnp.bfloat16)
    dv_low = dvalue.reshape(token_rows, kv_count * head_dim).astype(jnp.bfloat16)
    grad_query = outer_sum(normalized_input, dq_low)
    grad_key = outer_sum(normalized_input, dk_low)
    grad_value = outer_sum(normalized_input, dv_low)
    dnormed_part = (
        times_transposed(dq_low, full_query)
        + times_transposed(dk_low, full_key)
        + times_transposed(dv_low, full_value)
    )
    dnormed, grad_query_gain, grad_key_gain, grad_ffn_gain = (
        lax.psum(dnormed_part.astype(jnp.bfloat16), "tp").astype(jnp.float32),
        lax.psum(grad_query_gain.astype(jnp.bfloat16), "tp").astype(jnp.float32),
        lax.psum(grad_key_gain.astype(jnp.bfloat16), "tp").astype(jnp.float32),
        lax.psum(grad_ffn_gain.astype(jnp.bfloat16), "tp").astype(jnp.float32),
    )
    _, attn_norm_pull = jax.vjp(rms_norm, inputs, attn_gain32)
    dinput_norm, grad_attn_gain = attn_norm_pull(dnormed)
    input_grad = (dresidual + dinput_norm).astype(jnp.bfloat16)
    gradients = (
        grad_attn_gain,
        grad_query,
        grad_key,
        grad_value,
        grad_query_gain,
        grad_key_gain,
        grad_out,
        grad_ffn_gain,
        grad_gate,
        grad_up,
        grad_down,
    )
    grad_dims = (0, 0, 0, 0, 0, 0, 1, 0, 0, 0, 1)
    piece_count = fsdp_count * ctx_count
    packed = pack_grads(gradients, grad_dims, piece_count)
    reduced = lax.psum_scatter(
        packed.astype(jnp.bfloat16), ("fsdp", "ctx"), scatter_dimension=0, tiled=True
    ).astype(jnp.float32)
    collected_rows = lax.all_gather(reduced.astype(jnp.bfloat16), "ctx", axis=0, tiled=True).astype(
        reduced.dtype
    )
    collected = unpack_grads(collected_rows, gradients, grad_dims, piece_count)
    return (
        layer_low.reshape(seq_count, block_len, model_dim),
        input_grad.reshape(seq_count, block_len, model_dim),
        collected[0],
        collected[1],
        collected[2],
        collected[3],
        collected[4],
        collected[5],
        collected[6],
        collected[7],
        collected[8],
        collected[9],
        collected[10],
    )


def solution(mesh):
    placed = (
        P("fsdp", "ctx", None),
        P("fsdp"),
        P("fsdp", "tp"),
        P("fsdp", "tp"),
        P("fsdp", "tp"),
        P("fsdp"),
        P("fsdp"),
        P("tp", "fsdp"),
        P("fsdp"),
        P("fsdp", "tp"),
        P("fsdp", "tp"),
        P("tp", "fsdp"),
        P("fsdp"),
        P("fsdp", "ctx", None),
    )
    return jax.shard_map(
        shards,
        mesh=mesh,
        in_specs=placed,
        out_specs=(
            P("fsdp", "ctx", None),
            P("fsdp", "ctx", None),
            P("fsdp"),
            P("fsdp", "tp"),
            P("fsdp", "tp"),
            P("fsdp", "tp"),
            P("fsdp"),
            P("fsdp"),
            P("tp", "fsdp"),
            P("fsdp"),
            P("fsdp", "tp"),
            P("fsdp", "tp"),
            P("tp", "fsdp"),
        ),
        check_vma=False,
    )
```

profile of v0, /device:TPU:0, one launch (start us, length us, event | category | flops | bytes accessed | tf_op | source)
XLA Modules:
  0.0 1090.8 jit_solution(5404489563238779598)
XLA Ops:
  8.8 3.2 fusion.85
  12.7 6.2 all-gather
  18.9 8.2 all_gather.45
  34.2 7.3 all-reduce.9
  42.2 5.6 all_gather.47
  48.1 5.4 fusion.87
  53.5 5.8 all_gather.43
  60.8 6.9 all_gather.44
  70.8 3.8 multiply_reduce_fusion.6
  75.6 22.4 %while.39 = (s32[]{:T(128)}, f32[2,1,4,512]{3,2,0,1:T(4,128)S(1)}, f32[2,1,4,512]{3,2,0,1:T(4,128)S(1)}, s32[2]{0:T(128)S(1)}, s32[2]{0:T(128)S(1)}, /*index=5*/...) while((s32[]{:T(128)}, f32[2,1,4,512]{3,2,0,1:T(4,128)S(1)}, ...), condition=%wide.region_6.7_spmd.clone, body=%wide.region_3.6_spmd.clone.sunk | while | flops 283924480 | bytes 19755172 | solution.py:203
  77.5 4.9 fusion.189
  82.4 4.4 exponential_reduce_fusion.2
  88.7 4.9 fusion.189
  93.6 4.4 exponential_reduce_fusion.2
  98.7 11.8 %while.40 = (s32[]{:T(128)}, f32[2,512,1,4,64]{1,4,3,0,2:T(8,128)S(1)}, bf16[2,2,512,1,64]{2,4,1,3,0:T(8,128)(2,1)}, s32[2]{0:T(128)S(1)}, s32[2]{0:T(128)S(1)},...) while((s32[]{:T(128)}, ...), condition=%wide.region_8.9_spmd.clone, body=%wide.region_7.8_spmd.clone.sunk | while | flops 546572288 | bytes 4486311 | solution.py:222
  100.5 4.0 fusion.194
  106.4 4.0 fusion.194
  111.2 4.7 convolution_convert_fusion.1
  117.8 5.4 all-gather.1
  123.1 148.3 %all-reduce.15.cloned.1.call-done = bf16[1024,2048]{1,0:T(8,128)(2,1)} async-done(((bf16[1024,2048]{1,0:T(8,128)(2,1)}), bf16[1024,2048]{1,0:T(8,128)(2,1)}) %all-reduce.15.cloned.1.call-update) | async-done | bytes 4194320 | tf_op jit(solution)/shard_map/psum | solution.py:227
  271.4 5.0 multiply_reduce_fusion.1
  277.3 6.0 bitcast_add_fusion.1
  283.3 5.2 all-gather.14.cloned.1.call-done
  288.5 4.8 fusion.122
  293.3 13.3 %all-gather.16.cloned.1.call-done = bf16[2048,256]{1,0:T(8,128)(2,1)} async-done(((bf16[512,256]{1,0:T(8,128)(2,1)}), bf16[2048,256]{1,0:T(8,128)(2,1)}) %all-gather.16.cloned.1.call-update) | async-done | bytes 1048592 | tf_op jit(solution)/shard_map/all_gather | solution.py:119
  306.7 4.7 fusion.123
  311.4 13.4 %all-gather.18.cloned.1.call-done = bf16[256,2048]{1,0:T(8,128)(2,1)} async-done(((bf16[256,512]{1,0:T(8,128)(2,1)}), bf16[256,2048]{1,0:T(8,128)(2,1)}) %all-gather.18.cloned.1.call-update) | async-done | bytes 1048592 | tf_op jit(solution)/shard_map/all_gather | solution.py:120
  324.8 4.8 multiply_convert_fusion.1
  331.4 3.3 add_convert_fusion.1
  334.8 4.4 convolution_convert_fusion
  339.2 150.7 %all-reduce.17.cloned.1.call-done = bf16[1024,2048]{1,0:T(8,128)(2,1)} async-done(((bf16[1024,2048]{1,0:T(8,128)(2,1)}), bf16[1024,2048]{1,0:T(8,128)(2,1)}) %all-reduce.17.cloned.1.call-update) | async-done | bytes 4194320 | tf_op jit(solution)/shard_map/psum | solution.py:247
  489.9 6.8 multiply_reduce_fusion
  497.0 7.4 fusion.80
  504.5 3.3 copy-done.4
  513.0 46.1 %while.41 = (s32[]{:T(128)}, f32[2,512,1,4,64]{1,4,3,0,2:T(8,128)S(1)}, bf16[2,2,512,1,64]{2,4,1,3,0:T(8,128)(2,1)}, bf16[2,2,512,1,64]{2,4,1,3,0:T(8,128)(2,1)}...) while((s32[]{:T(128)}, ...), condition=%wide.region_16.17_spmd.clone, body=%wide.region_15.16_spmd.clone.sunk | while | flops 1364789248 | bytes 100594080 | solution.py:281
  516.2 3.3 copy-done.5
  519.5 5.1 fusion.206
  524.6 3.2 fusion.207
  529.5 5.7 fusion.209
  539.1 3.3 copy-done.5
  542.4 5.1 fusion.206
  547.5 3.2 fusion.207
  552.4 5.7 fusion.209
  566.9 10.8 reduce-scatter.2.cloned.1.call-done
  582.6 3.3 add_convert_fusion
  587.0 3.5 convolution_convert_fusion.4
  591.0 4.2 convolution_convert_fusion.3
  596.7 4.4 fusion.90
  606.1 3.3 convert_element_type.210
  611.5 3.6 convolution_convert_fusion.6
  616.5 4.7 convolution_convert_fusion.5
  622.8 3.0 convolution_convert_fusion.8
  630.4 13.4 %all-reduce.7 = (bf16[8,8]{1,0:T(8,128)(2,1)S(1)}, bf16[8,8]{1,0:T(8,128)(2,1)S(1)}, bf16[8,256]{1,0:T(8,128)(2,1)S(1)}) all-reduce(bf16[8,8]{1,0:T(8,128)(2,1)S(1)} %reshape.780, bf16[8,8]{1,0:T(8,128)(2,1)S(1)} %reshape.781, bf16[8,256]{1,0:T(8,128)(2,1)S(1)} %reshape.783), channel_id=1, replica_groups=mesh['fsdp'=4,'ctx'=2,'tp'=4] {'tp'}, use_global_device_ids=true, to_apply=%region_24.25 | all-reduce | flops 2176 | bytes 8704 | tf_op jit(solution)/shard_map/psum | solution.py:308
  643.8 233.6 %all-reduce.21.cloned.1.call-done = (bf16[1024,2048]{1,0:T(8,128)(2,1)}, bf16[1024,2048]{1,0:T(8,128)(2,1)}) async-done(((bf16[1024,2048]{1,0:T(8,128)(2,1)}, bf16[1024,2048]{1,0:T(8,128)(2,1)}), (bf16[1024,2048]{1,0:T(8,128)(2,1)}, bf16[1024,2048]{1,0:T(8,128)(2,1)})) %all-reduce.21.cloned.1.call-update) | async-done | bytes 8388624 | tf_op jit(solution)/shard_map/psum | solution.py:236
  877.5 5.9 fusion.79
  890.5 7.1 dynamic-update-slice.8
  899.0 6.8 dynamic-update-slice.10
  905.8 6.8 dynamic-update-slice.11
  912.6 6.7 dynamic-update-slice.12
  920.1 97.4 %all-reduce.19.cloned.1.call-done = bf16[8,360976]{1,0:T(8,128)(2,1)} async-done(((bf16[8,360976]{1,0:T(8,128)(2,1)}), bf16[8,360976]{1,0:T(8,128)(2,1)}) %all-reduce.19.cloned.1.call-update) | async-done | bytes 5775632
  1017.4 6.1 dynamic-slice_bitcast_fusion
  1023.6 14.9 %fusion.82 = (bf16[1024,2048]{1,0:T(8,128)(2,1)}, bf16[1024,2048]{1,0:T(8,128)(2,1)}) fusion(f32[1024,2048]{1,0:T(8,128)} %copy-done.4, bf16[1024,2048]{1,0:T(8,128)(2,1)} %get-tuple-element.498, bf16[2,512,2048]{2,1,0:T(8,128)(2,1)} %param.20, f32[1024]{0:T(1024)S(1)} %multiply_multiply_fusion.3, f32[2048]{0:T(1024)S(1)} %bitcast.468, ...), kind=kLoop, calls=%fused_computation.93 | loop fusion | flops 29360128 | bytes 33570816 | tf_op jit(solution)/shard_map/convert_element_type | solution.py:314
  1038.5 27.2 %all-gather.20.cloned.1.call-done = bf16[2,1,360976]{2,1,0:T(2,128)(2,1)} async-done(((bf16[1,1,360976]{2,1,0:T(2,128)(2,1)}), bf16[2,1,360976]{2,1,0:T(2,128)(2,1)}) %all-gather.20.cloned.1.call-update) | async-done | bytes 1443920 | tf_op jit(solution)/shard_map/all_gather | solution.py:334
  1065.7 5.0 copy.153
  (338 shorter events, 93.2 us)
Async XLA Ops:
  7.2 61.4 %all-gather.10.cloned.1.call-start = ((), (), s32[]{:S(2)}) async-start(), calls=%async_computation.1 | async-start | bytes 1310720 | tf_op jit(solution)/shard_map/all_gather | solution.py:111
  7.9 103.3 %all-gather.12.cloned.1.call-start = ((), (), s32[]{:S(2)}) async-start(), calls=%async_computation.2 | async-start | bytes 1310720 | tf_op jit(solution)/shard_map/all_gather | solution.py:116
  8.7 262.8 %all-reduce.15.cloned.1.call-start = ((), (), s32[]{:S(2)}) async-start(), calls=%async_computation.3 | async-start | bytes 8388608 | tf_op jit(solution)/shard_map/psum | solution.py:227
  8.8 18.3 %copy-start.1 = (bf16[2,512,2048]{2,1,0:T(8,128)(2,1)S(1)}, bf16[2,512,2048]{2,1,0:T(8,128)(2,1)}, u32[]{:S(2)}) copy-start(bf16[2,512,2048]{2,1,0:T(8,128)(2,1)} %param.20) | copy-start | bytes 12582916
  12.0 19.6 %copy-start.51 = (f32[1,4,2,128]{3,1,2,0:T(4,128)}, f32[1,4,2,128]{3,1,2,0:T(4,128)S(1)}, u32[]{:S(2)}) copy-start(f32[1,4,2,128]{3,1,2,0:T(4,128)S(1)} %copy.136) | copy-start | bytes 12292
  12.0 19.6 %copy-start.49 = (f32[1024]{0:T(1024)}, f32[1024]{0:T(1024)S(1)}, u32[]{:S(2)}) copy-start(f32[1024]{0:T(1024)S(1)} %rsqrt.54) | copy-start | bytes 12292
  18.9 29.2 %copy-start.41 = (f32[4,1,512]{2,1,0:T(1,128)}, f32[4,1,512]{2,1,0:T(1,128)S(1)}, u32[]{:S(2)}) copy-start(f32[4,1,512]{2,1,0:T(1,128)S(1)} %convert_element_type.229) | copy-start | bytes 24580
  27.1 4.5 copy-start.23
  27.1 5.4 copy-start.64
  27.1 6.6 copy-start.61
  27.1 6.9 copy-start.62
  32.2 21.2 %copy-start.44 = (f32[2,512]{1,0:T(2,128)}, f32[2,512]{1,0:T(2,128)S(1)}, u32[]{:S(2)}) copy-start(f32[2,512]{1,0:T(2,128)S(1)} %rsqrt.55) | copy-start | bytes 12292
  32.5 21.0 %copy-start.12 = (f32[2,512,1,64]{1,0,3,2:T(2,128)}, f32[2,512,1,64]{1,0,3,2:T(2,128)S(1)}, u32[]{:S(2)}) copy-start(f32[2,512,1,64]{1,0,3,2:T(2,128)S(1)} %reshape.768) | copy-start | bytes 786436
  41.6 11.9 %copy-start.55 = (f32[64]{0:T(128)}, f32[64]{0:T(128)S(1)}, u32[]{:S(2)}) copy-start(f32[64]{0:T(128)S(1)} %convert_element_type.189) | copy-start | bytes 772
  41.7 11.8 %copy-start.46 = (bf16[512,64]{0,1:T(8,128)(2,1)S(1)}, bf16[512,64]{0,1:T(8,128)(2,1)}, u32[]{:S(2)}) copy-start(bf16[512,64]{0,1:T(8,128)(2,1)} %param.24) | copy-start | bytes 196612
  42.0 33.0 %copy-start.19 = (f32[512,64]{0,1:T(8,128)}, f32[512,64]{0,1:T(8,128)S(1)}, u32[]{:S(2)}) copy-start(f32[512,64]{0,1:T(8,128)S(1)} %get-tuple-element.546) | copy-start | bytes 393220
  42.1 33.0 %copy-start.21 = (f32[512,64]{0,1:T(8,128)}, f32[512,64]{0,1:T(8,128)S(1)}, u32[]{:S(2)}) copy-start(f32[512,64]{0,1:T(8,128)S(1)} %get-tuple-element.545) | copy-start | bytes 393220
  48.0 11.2 %copy-start.9 = (bf16[1024,2048]{1,0:T(8,128)(2,1)S(1)}, bf16[1024,2048]{1,0:T(8,128)(2,1)}, u32[]{:S(2)}) copy-start(bf16[1024,2048]{1,0:T(8,128)(2,1)} %copy-done.8) | copy-start | bytes 12582916
  53.5 21.6 %copy-start.57 = (f32[64]{0:T(128)}, f32[64]{0:T(128)S(1)}, u32[]{:S(2)}) copy-start(f32[64]{0:T(128)S(1)} %convert_element_type.194) | copy-start | bytes 772
  59.3 15.4 %copy-start.25 = (bf16[2048,64]{0,1:T(8,128)(2,1)}, bf16[2048,64]{0,1:T(8,128)(2,1)S(1)}, u32[]{:S(2)}) copy-start(bf16[2048,64]{0,1:T(8,128)(2,1)S(1)} %all_gather.43) | copy-start | bytes 786436
  111.1 4.8 copy-start.14
  111.2 6.5 copy-start.60
  115.9 172.6 %all-gather.14.cloned.1.call-start = ((), (), s32[]{:S(2)}) async-start(), calls=%async_computation.4 | async-start | bytes 1310720 | tf_op jit(solution)/shard_map/all_gather | solution.py:118
  116.5 190.1 %all-gather.16.cloned.1.call-start = ((), (), s32[]{:S(2)}) async-start(), calls=%async_computation.5 | async-start | bytes 1310720 | tf_op jit(solution)/shard_map/all_gather | solution.py:119
  117.1 207.7 %all-gather.18.cloned.1.call-start = ((), (), s32[]{:S(2)}) async-start(), calls=%async_computation.6 | async-start | bytes 1310720 | tf_op jit(solution)/shard_map/all_gather | solution.py:120
  117.7 372.2 %all-reduce.17.cloned.1.call-start = ((), (), s32[]{:S(2)}) async-start(), calls=%async_computation.7 | async-start | bytes 8388608 | tf_op jit(solution)/shard_map/psum | solution.py:247
  271.4 5.0 copy-start.2
  271.4 5.9 copy-start.6
  324.8 4.8 copy-start.29
  329.6 5.2 copy-start.27
  334.7 243.0 %reduce-scatter.2.cloned.1.call-start = ((), (), s32[]{:S(2)}) async-start(), calls=%async_computation.8 | async-start | bytes 786432 | tf_op jit(solution)/shard_map/reduce_scatter | solution.py:287
  489.9 6.8 copy-start.3
  489.9 7.1 copy-start.7
  497.0 10.8 copy-start.18
  513.0 46.2 %copy-start.20 = (f32[512,64]{0,1:T(8,128)S(1)}, f32[512,64]{0,1:T(8,128)}, u32[]{:S(2)}) copy-start(f32[512,64]{0,1:T(8,128)} %copy-done.19) | copy-start | bytes 393220
  513.0 6.5 copy-start.36
  524.6 4.9 copy-start.39
  524.6 3.5 copy-start
  529.5 5.7 copy-start.38
  535.9 6.5 copy-start.36
  547.5 4.9 copy-start.39
  547.5 3.5 copy-start
  552.4 5.7 copy-start.38
  559.1 6.2 copy-start.11
  559.1 6.2 copy-start.22
  559.2 6.2 copy-start.35
  559.2 6.2 copy-start.58
  559.2 6.8 copy-start.48
  564.0 313.5 %all-reduce.21.cloned.1.call-start = ((), (), s32[]{:S(2)}) async-start(), calls=%async_computation.11 | async-start | bytes 16777216 | tf_op jit(solution)/shard_map/psum | solution.py:236
  565.3 13.5 %copy-start.13 = (f32[2,512,1,64]{1,0,3,2:T(2,128)S(1)}, f32[2,512,1,64]{1,0,3,2:T(2,128)}, u32[]{:S(2)}) copy-start(f32[2,512,1,64]{1,0,3,2:T(2,128)} %copy-done.12) | copy-start | bytes 786436
  565.3 13.5 %copy-start.45 = (f32[2,512]{1,0:T(2,128)S(1)}, f32[2,512]{1,0:T(2,128)}, u32[]{:S(2)}) copy-start(f32[2,512]{1,0:T(2,128)} %copy-done.44) | copy-start | bytes 12292
  565.3 13.5 %copy-start.56 = (f32[64]{0:T(128)S(1)}, f32[64]{0:T(128)}, u32[]{:S(2)}) copy-start(f32[64]{0:T(128)} %copy-done.55) | copy-start | bytes 772
  565.4 14.2 %copy-start.54 = (f32[2,512]{1,0:T(2,128)S(1)}, f32[2,512]{1,0:T(2,128)}, u32[]{:S(2)}) copy-start(f32[2,512]{1,0:T(2,128)} %copy-done.53) | copy-start | bytes 12292
  565.4 14.5 %copy-start.24 = (bf16[2048,64]{0,1:T(8,128)(2,1)S(1)}, bf16[2048,64]{0,1:T(8,128)(2,1)}, u32[]{:S(2)}) copy-start(bf16[2048,64]{0,1:T(8,128)(2,1)} %copy-done.23) | copy-start | bytes 786436
  586.0 431.4 %all-reduce.19.cloned.1.call-start = ((), (), s32[]{:S(2)}) async-start(), calls=%async_computation.10 | async-start | bytes 11554816
  591.0 5.7 copy-start.28
  611.4 5.2 copy-start.15
  616.5 6.2 copy-start.59
  622.8 254.7 %copy-start.42 = (f32[4,1,512]{2,1,0:T(1,128)S(1)}, f32[4,1,512]{2,1,0:T(1,128)}, u32[]{:S(2)}) copy-start(f32[4,1,512]{2,1,0:T(1,128)} %copy-done.41) | copy-start | bytes 24580
  622.8 254.7 %copy-start.50 = (f32[1024]{0:T(1024)S(1)}, f32[1024]{0:T(1024)}, u32[]{:S(2)}) copy-start(f32[1024]{0:T(1024)} %copy-done.49) | copy-start | bytes 12292
  883.4 22.5 %copy-start.17 = (bf16[8,65536]{1,0:T(8,128)(2,1)S(1)}, bf16[8,65536]{1,0:T(8,128)(2,1)}, u32[]{:S(2)}) copy-start(bf16[8,65536]{1,0:T(8,128)(2,1)} %reshape.785) | copy-start | bytes 3145732
  899.0 20.4 %copy-start.63 = (u32[32]{0:T(128)S(1)}, u32[32]{0:T(128)}, u32[]{:S(2)}) copy-start(u32[32]{0:T(128)} %constant.133) | copy-start | bytes 388
  912.6 110.9 %copy-start.52 = (f32[1,4,2,128]{3,1,2,0:T(4,128)S(1)}, f32[1,4,2,128]{3,1,2,0:T(4,128)}, u32[]{:S(2)}) copy-start(f32[1,4,2,128]{3,1,2,0:T(4,128)} %copy-done.51) | copy-start | bytes 12292
  919.4 146.3 %all-gather.20.cloned.1.call-start = ((), (), s32[]{:S(2)}) async-start(), calls=%async_computation.9 | async-start | bytes 4333056 | tf_op jit(solution)/shard_map/all_gather | solution.py:334
  (20 other events, 34.2 us)
Sparse Core Ops, SparseCore 0:
  9.5 20.8 all-gather.9
  32.0 16.6 all-gather.11
  116.1 155.3 all-reduce.14
  272.8 15.6 all-gather.13
  289.9 16.6 all-gather.15
  308.1 16.6 all-gather.17
  334.9 154.9 all-reduce.16
  564.1 13.5 reduce-scatter.1
  586.1 291.3 all-reduce.20
  919.5 97.8 all-reduce.18
  1023.7 41.9 all-gather.19
where the time goes:
time: 1100 us; the launch traced here: 1090 us
  waiting for transfers between devices  703 us (64%)
  matrix products  119 us (11%)
  local copies, waits for them, and re-layouts  104 us (9%)
  other arithmetic  84.2 us (8%)
  blocking collectives  58.7 us (5%)
  between operations  16 us (1%)
    psum x1, waiting for transfers between devices, shards(): lax.psum(ffn_part.astype(jnp.bfloat16), 'tp').astype(jnp.float32)  234 us
    psum x1, waiting for transfers between devices, shards(): dffn_in = lax.psum(dffn_part.astype(jnp.bfloat16), 'tp').astype(jnp.float32)  151 us
    psum x1, waiting for transfers between devices, shards(): lax.psum(attn_part.astype(jnp.bfloat16), 'tp').astype(jnp.float32)  148 us
    unnamed x12, waiting for transfers between devices  100 us
    unnamed x152, local copies, waits for them, and re-layouts  57.9 us
    all_gather x1, waiting for transfers between devices, shards(): lax.all_gather(reduced.astype(jnp.bfloat16), 'ctx', axis=0, tiled=True)  27.2 us
    dot_general x7, matrix products, outer_sum(): lax.dot_general(left, right, (((0,), (0,)), ((), ())), preferred_element_...  26.6 us
  transfers between devices with their start and end apart: 11, of which 9 were waited for; matrix products, arithmetic and copies ran while one was open for 13% of the time, Pallas kernels for 0%

commit v1 on v0

--- a/solution.py
+++ b/solution.py
@@ -244,7 +244,9 @@
     grad_gate = outer_sum(ffn_in, dgate)
     grad_up = outer_sum(ffn_in, dup)
     dffn_part = times_transposed(dgate, full_gate) + times_transposed(dup, full_up)
-    dffn_in = lax.psum(dffn_part.astype(jnp.bfloat16), "tp").astype(jnp.float32)
+    dffn_in = jnp.sum(lax.all_gather(dffn_part.astype(jnp.bfloat16), "tp"), axis=0).astype(
+        jnp.float32
+    )
     _, ffn_norm_pull = jax.vjp(rms_norm, residual, ffn_gain32)
     dres_norm, _ = ffn_norm_pull(dffn_in)
     dresidual = grad_low.astype(jnp.float32) + dres_norm

time: 1100 us -> 1240 us (1.13)
  waiting for transfers between devices: 703 us -> 833 us
    all_gather x0 -> x1, waiting for transfers between devices: none -> 282 us  [shards(): lax.all_gather(dffn_part.astype(jnp.bfloat16), 'tp')]
    psum x1 -> x0, waiting for transfers between devices: 151 us -> none  [shards(): dffn_in = lax.psum(dffn_part.astype(jnp.bfloat16), 'tp').astype(jnp.float32)]
  transfers between devices with their start and end apart: 11 -> 11, of which waited for: 9 -> 9; matrix products, arithmetic and copies ran while one was open for 13% -> 12% of each run, Pallas kernels for 0% -> 0%
where the time goes in v1:
time: 1240 us; the launch traced here: 1230 us
  waiting for transfers between devices  833 us (67%)
  matrix products  119 us (10%)
  local copies, waits for them, and re-layouts  105 us (8%)
  other arithmetic  96.2 us (8%)
  blocking collectives  58.1 us (5%)
  between operations  16 us (1%)
    all_gather x1, waiting for transfers between devices, shards(): lax.all_gather(dffn_part.astype(jnp.bfloat16), 'tp')  282 us
    psum x1, waiting for transfers between devices, shards(): lax.psum(ffn_part.astype(jnp.bfloat16), 'tp').astype(jnp.float32)  234 us
    psum x1, waiting for transfers between devices, shards(): lax.psum(attn_part.astype(jnp.bfloat16), 'tp').astype(jnp.float32)  148 us
    unnamed x12, waiting for transfers between devices  100 us
    unnamed x152, local copies, waits for them, and re-layouts  57.8 us
    all_gather x1, waiting for transfers between devices, shards(): lax.all_gather(reduced.astype(jnp.bfloat16), 'ctx', axis=0, tiled=True)  27.2 us
    dot_general x7, matrix products, outer_sum(): lax.dot_general(left, right, (((0,), (0,)), ((), ())), preferred_element_...  26.6 us
  transfers between devices with their start and end apart: 11, of which 9 were waited for; matrix products, arithmetic and copies ran while one was open for 12% of the time, Pallas kernels for 0%

profile of v1, /device:TPU:0, one launch (start us, length us, event | category | flops | bytes accessed | tf_op | source)
XLA Modules:
  0.0 1233.2 jit_solution(16332656233213846107)
XLA Ops:
  8.8 3.2 fusion.85
  12.7 6.2 all-gather.1
  18.9 8.2 all_gather.51
  34.2 7.3 all-reduce.9
  42.2 5.6 all_gather.53
  48.1 5.4 fusion.87
  53.5 5.8 all_gather.49
  60.8 6.6 all_gather.50
  70.5 3.8 multiply_reduce_fusion.6
  75.3 22.4 %while.39 = (s32[]{:T(128)}, f32[2,1,4,512]{3,2,0,1:T(4,128)S(1)}, f32[2,1,4,512]{3,2,0,1:T(4,128)S(1)}, s32[2]{0:T(128)S(1)}, s32[2]{0:T(128)S(1)}, /*index=5*/...) while((s32[]{:T(128)}, f32[2,1,4,512]{3,2,0,1:T(4,128)S(1)}, ...), condition=%wide.region_6.7_spmd.clone, body=%wide.region_3.6_spmd.clone.sunk | while | flops 283924480 | bytes 19755172 | solution.py:203
  77.2 4.9 fusion.189
  82.1 4.4 exponential_reduce_fusion.2
  88.4 4.9 fusion.189
  93.3 4.4 exponential_reduce_fusion.2
  98.3 11.8 while.40
  100.2 4.0 fusion.194
  106.1 4.0 fusion.194
  110.9 4.7 convolution_convert_fusion.1
  117.4 5.4 all-gather.2
  122.8 148.2 %all-reduce.14.cloned.1.call-done = bf16[1024,2048]{1,0:T(8,128)(2,1)} async-done(((bf16[1024,2048]{1,0:T(8,128)(2,1)}), bf16[1024,2048]{1,0:T(8,128)(2,1)}) %all-reduce.14.cloned.1.call-update) | async-done | bytes 4194320 | tf_op jit(solution)/shard_map/psum | solution.py:227
  271.1 5.0 multiply_reduce_fusion.1
  277.0 6.0 bitcast_add_fusion.1
  283.0 5.2 all-gather.16.cloned.1.call-done
  288.2 4.7 fusion.122
  292.9 13.4 %all-gather.18.cloned.1.call-done = bf16[2048,256]{1,0:T(8,128)(2,1)} async-done(((bf16[512,256]{1,0:T(8,128)(2,1)}), bf16[2048,256]{1,0:T(8,128)(2,1)}) %all-gather.18.cloned.1.call-update) | async-done | bytes 1048592 | tf_op jit(solution)/shard_map/all_gather | solution.py:119
  306.3 4.7 fusion.123
  311.0 13.4 %all-gather.20.cloned.1.call-done = bf16[256,2048]{1,0:T(8,128)(2,1)} async-done(((bf16[256,512]{1,0:T(8,128)(2,1)}), bf16[256,2048]{1,0:T(8,128)(2,1)}) %all-gather.20.cloned.1.call-update) | async-done | bytes 1048592 | tf_op jit(solution)/shard_map/all_gather | solution.py:120
  324.5 4.8 multiply_convert_fusion.1
  331.0 3.4 add_convert_fusion.1
  334.9 4.4 convolution_convert_fusion
  339.4 282.0 %all-gather.22.cloned.1.call-done = bf16[4096,2048]{1,0:T(8,128)(2,1)} async-done(((bf16[1024,2048]{1,0:T(8,128)(2,1)}), bf16[4096,2048]{1,0:T(8,128)(2,1)}) %all-gather.22.cloned.1.call-update) | async-done | bytes 16777232 | tf_op jit(solution)/shard_map/all_gather | solution.py:247
  621.4 12.2 reduce_sum.161
  633.6 6.8 multiply_reduce_fusion
  640.7 7.2 fusion.80
  647.9 3.3 copy-done.4
  656.5 45.8 %while.41 = (s32[]{:T(128)}, f32[2,512,1,4,64]{1,4,3,0,2:T(8,128)S(1)}, bf16[2,2,512,1,64]{2,4,1,3,0:T(8,128)(2,1)}, bf16[2,2,512,1,64]{2,4,1,3,0:T(8,128)(2,1)}...) while((s32[]{:T(128)}, ...), condition=%wide.region_16.17_spmd.clone, body=%wide.region_15.16_spmd.clone.sunk | while | flops 1364789248 | bytes 100594080 | solution.py:283
  659.8 3.3 copy-done.5
  663.1 5.1 fusion.206
  668.2 3.2 fusion.207
  673.1 5.7 fusion.209
  682.6 3.3 copy-done.5
  685.9 5.1 fusion.206
  691.0 3.2 fusion.207
  695.9 5.7 fusion.209
  710.3 9.8 reduce-scatter.2.cloned.1.call-done
  725.0 3.5 add_convert_fusion
  729.5 3.5 convolution_convert_fusion.4
  733.5 4.2 convolution_convert_fusion.3
  739.2 4.4 fusion.90
  748.8 3.3 convert_element_type.212
  754.2 3.6 convolution_convert_fusion.6
  759.3 4.7 convolution_convert_fusion.5
  773.2 13.1 %all-reduce.7 = (bf16[8,8]{1,0:T(8,128)(2,1)S(1)}, bf16[8,8]{1,0:T(8,128)(2,1)S(1)}, bf16[8,256]{1,0:T(8,128)(2,1)S(1)}) all-reduce(bf16[8,8]{1,0:T(8,128)(2,1)S(1)} %reshape.780, bf16[8,8]{1,0:T(8,128)(2,1)S(1)} %reshape.781, bf16[8,256]{1,0:T(8,128)(2,1)S(1)} %reshape.783), channel_id=1, replica_groups=mesh['fsdp'=4,'ctx'=2,'tp'=4] {'tp'}, use_global_device_ids=true, to_apply=%region_24.25 | all-reduce | flops 2176 | bytes 8704 | tf_op jit(solution)/shard_map/psum | solution.py:310
  786.3 233.7 %all-reduce.18.cloned.1.call-done = (bf16[1024,2048]{1,0:T(8,128)(2,1)}, bf16[1024,2048]{1,0:T(8,128)(2,1)}) async-done(((bf16[1024,2048]{1,0:T(8,128)(2,1)}, bf16[1024,2048]{1,0:T(8,128)(2,1)}), (bf16[1024,2048]{1,0:T(8,128)(2,1)}, bf16[1024,2048]{1,0:T(8,128)(2,1)})) %all-reduce.18.cloned.1.call-update) | async-done | bytes 8388624 | tf_op jit(solution)/shard_map/psum | solution.py:236
  1020.0 5.9 fusion.79
  1032.9 7.1 dynamic-update-slice.8
  1041.5 6.8 dynamic-update-slice.10
  1048.3 6.8 dynamic-update-slice.11
  1055.1 6.8 dynamic-update-slice.12
  1062.5 97.4 %all-reduce.16.cloned.1.call-done = bf16[8,360976]{1,0:T(8,128)(2,1)} async-done(((bf16[8,360976]{1,0:T(8,128)(2,1)}), bf16[8,360976]{1,0:T(8,128)(2,1)}) %all-reduce.16.cloned.1.call-update) | async-done | bytes 5775632
  1159.9 6.1 dynamic-slice_bitcast_fusion
  1166.0 14.9 %fusion.82 = (bf16[1024,2048]{1,0:T(8,128)(2,1)}, bf16[1024,2048]{1,0:T(8,128)(2,1)}) fusion(f32[1024,2048]{1,0:T(8,128)} %copy-done.4, bf16[1024,2048]{1,0:T(8,128)(2,1)} %get-tuple-element.498, bf16[2,512,2048]{2,1,0:T(8,128)(2,1)} %param.20, f32[1024]{0:T(1024)S(1)} %multiply_multiply_fusion.3, f32[2048]{0:T(1024)S(1)} %bitcast.470, ...), kind=kLoop, calls=%fused_computation.93 | loop fusion | flops 29360128 | bytes 33570816 | tf_op jit(solution)/shard_map/convert_element_type | solution.py:316
  1180.9 27.2 %all-gather.24.cloned.1.call-done = bf16[2,1,360976]{2,1,0:T(2,128)(2,1)} async-done(((bf16[1,1,360976]{2,1,0:T(2,128)(2,1)}), bf16[2,1,360976]{2,1,0:T(2,128)(2,1)}) %all-gather.24.cloned.1.call-update) | async-done | bytes 1443920 | tf_op jit(solution)/shard_map/all_gather | solution.py:336
  1208.2 5.0 copy.153
  (339 shorter events, 97.1 us)
Async XLA Ops:
  7.2 61.1 %all-gather.12.cloned.1.call-start = ((), (), s32[]{:S(2)}) async-start(), calls=%async_computation.1 | async-start | bytes 1310720 | tf_op jit(solution)/shard_map/all_gather | solution.py:111
  7.9 102.9 %all-gather.14.cloned.1.call-start = ((), (), s32[]{:S(2)}) async-start(), calls=%async_computation.2 | async-start | bytes 1310720 | tf_op jit(solution)/shard_map/all_gather | solution.py:116
  8.7 262.4 %all-reduce.14.cloned.1.call-start = ((), (), s32[]{:S(2)}) async-start(), calls=%async_computation.3 | async-start | bytes 8388608 | tf_op jit(solution)/shard_map/psum | solution.py:227
  8.8 18.3 %copy-start.1 = (bf16[2,512,2048]{2,1,0:T(8,128)(2,1)S(1)}, bf16[2,512,2048]{2,1,0:T(8,128)(2,1)}, u32[]{:S(2)}) copy-start(bf16[2,512,2048]{2,1,0:T(8,128)(2,1)} %param.20) | copy-start | bytes 12582916
  12.0 19.6 %copy-start.51 = (f32[1,4,2,128]{3,1,2,0:T(4,128)}, f32[1,4,2,128]{3,1,2,0:T(4,128)S(1)}, u32[]{:S(2)}) copy-start(f32[1,4,2,128]{3,1,2,0:T(4,128)S(1)} %copy.136) | copy-start | bytes 12292
  12.0 19.6 %copy-start.49 = (f32[1024]{0:T(1024)}, f32[1024]{0:T(1024)S(1)}, u32[]{:S(2)}) copy-start(f32[1024]{0:T(1024)S(1)} %rsqrt.54) | copy-start | bytes 12292
  18.9 29.2 %copy-start.41 = (f32[4,1,512]{2,1,0:T(1,128)}, f32[4,1,512]{2,1,0:T(1,128)S(1)}, u32[]{:S(2)}) copy-start(f32[4,1,512]{2,1,0:T(1,128)S(1)} %convert_element_type.231) | copy-start | bytes 24580
  27.1 4.5 copy-start.23
  27.1 5.4 copy-start.64
  27.1 6.6 copy-start.61
  27.1 6.9 copy-start.62
  32.2 21.2 %copy-start.44 = (f32[2,512]{1,0:T(2,128)}, f32[2,512]{1,0:T(2,128)S(1)}, u32[]{:S(2)}) copy-start(f32[2,512]{1,0:T(2,128)S(1)} %rsqrt.55) | copy-start | bytes 12292
  32.5 21.0 %copy-start.12 = (f32[2,512,1,64]{1,0,3,2:T(2,128)}, f32[2,512,1,64]{1,0,3,2:T(2,128)S(1)}, u32[]{:S(2)}) copy-start(f32[2,512,1,64]{1,0,3,2:T(2,128)S(1)} %reshape.768) | copy-start | bytes 786436
  41.6 11.9 copy-start.55
  41.7 11.8 copy-start.46
  42.0 32.7 %copy-start.19 = (f32[512,64]{0,1:T(8,128)}, f32[512,64]{0,1:T(8,128)S(1)}, u32[]{:S(2)}) copy-start(f32[512,64]{0,1:T(8,128)S(1)} %get-tuple-element.546) | copy-start | bytes 393220
  42.1 32.7 %copy-start.21 = (f32[512,64]{0,1:T(8,128)}, f32[512,64]{0,1:T(8,128)S(1)}, u32[]{:S(2)}) copy-start(f32[512,64]{0,1:T(8,128)S(1)} %get-tuple-element.545) | copy-start | bytes 393220
  48.0 11.2 copy-start.9
  53.5 21.3 %copy-start.57 = (f32[64]{0:T(128)}, f32[64]{0:T(128)S(1)}, u32[]{:S(2)}) copy-start(f32[64]{0:T(128)S(1)} %convert_element_type.196) | copy-start | bytes 772
  59.3 15.1 %copy-start.25 = (bf16[2048,64]{0,1:T(8,128)(2,1)}, bf16[2048,64]{0,1:T(8,128)(2,1)S(1)}, u32[]{:S(2)}) copy-start(bf16[2048,64]{0,1:T(8,128)(2,1)S(1)} %all_gather.49) | copy-start | bytes 786436
  110.8 4.8 copy-start.14
  110.8 6.5 copy-start.60
  115.6 172.6 %all-gather.16.cloned.1.call-start = ((), (), s32[]{:S(2)}) async-start(), calls=%async_computation.4 | async-start | bytes 1310720 | tf_op jit(solution)/shard_map/all_gather | solution.py:118
  116.2 190.1 %all-gather.18.cloned.1.call-start = ((), (), s32[]{:S(2)}) async-start(), calls=%async_computation.5 | async-start | bytes 1310720 | tf_op jit(solution)/shard_map/all_gather | solution.py:119
  116.8 207.7 %all-gather.20.cloned.1.call-start = ((), (), s32[]{:S(2)}) async-start(), calls=%async_computation.6 | async-start | bytes 1310720 | tf_op jit(solution)/shard_map/all_gather | solution.py:120
  117.3 504.0 %all-gather.22.cloned.1.call-start = ((), (), s32[]{:S(2)}) async-start(), calls=%async_computation.8 | async-start | bytes 20971520 | tf_op jit(solution)/shard_map/all_gather | solution.py:247
  271.1 5.0 copy-start.2
  271.1 5.9 copy-start.6
  324.5 4.8 copy-start.29
  329.3 5.7 copy-start.27
  334.4 385.6 %reduce-scatter.2.cloned.1.call-start = ((), (), s32[]{:S(2)}) async-start(), calls=%async_computation.7 | async-start | bytes 786432 | tf_op jit(solution)/shard_map/reduce_scatter | solution.py:289
  633.5 6.8 copy-start.3
  633.5 7.1 copy-start.7
  640.7 10.6 copy-start.18
  656.5 45.9 %copy-start.20 = (f32[512,64]{0,1:T(8,128)S(1)}, f32[512,64]{0,1:T(8,128)}, u32[]{:S(2)}) copy-start(f32[512,64]{0,1:T(8,128)} %copy-done.19) | copy-start | bytes 393220
  656.6 6.5 copy-start.36
  668.2 4.9 copy-start.39
  668.2 3.5 copy-start
  673.1 5.7 copy-start.38
  679.5 6.5 copy-start.36
  691.0 4.9 copy-start.39
  691.0 3.5 copy-start
  695.9 5.7 copy-start.38
  702.3 6.4 copy-start.11
  702.3 6.4 copy-start.22
  702.3 6.4 copy-start.35
  702.3 6.4 copy-start.58
  702.3 7.0 copy-start.48
  707.1 312.9 %all-reduce.18.cloned.1.call-start = ((), (), s32[]{:S(2)}) async-start(), calls=%async_computation.11 | async-start | bytes 16777216 | tf_op jit(solution)/shard_map/psum | solution.py:236
  708.7 12.5 %copy-start.13 = (f32[2,512,1,64]{1,0,3,2:T(2,128)S(1)}, f32[2,512,1,64]{1,0,3,2:T(2,128)}, u32[]{:S(2)}) copy-start(f32[2,512,1,64]{1,0,3,2:T(2,128)} %copy-done.12) | copy-start | bytes 786436
  708.7 12.5 %copy-start.45 = (f32[2,512]{1,0:T(2,128)S(1)}, f32[2,512]{1,0:T(2,128)}, u32[]{:S(2)}) copy-start(f32[2,512]{1,0:T(2,128)} %copy-done.44) | copy-start | bytes 12292
  708.7 12.5 %copy-start.56 = (f32[64]{0:T(128)S(1)}, f32[64]{0:T(128)}, u32[]{:S(2)}) copy-start(f32[64]{0:T(128)} %copy-done.55) | copy-start | bytes 772
  708.7 13.2 %copy-start.54 = (f32[2,512]{1,0:T(2,128)S(1)}, f32[2,512]{1,0:T(2,128)}, u32[]{:S(2)}) copy-start(f32[2,512]{1,0:T(2,128)} %copy-done.53) | copy-start | bytes 12292
  708.7 13.5 %copy-start.24 = (bf16[2048,64]{0,1:T(8,128)(2,1)S(1)}, bf16[2048,64]{0,1:T(8,128)(2,1)}, u32[]{:S(2)}) copy-start(bf16[2048,64]{0,1:T(8,128)(2,1)} %copy-done.23) | copy-start | bytes 786436
  728.5 431.4 %all-reduce.16.cloned.1.call-start = ((), (), s32[]{:S(2)}) async-start(), calls=%async_computation.10 | async-start | bytes 11554816
  733.5 5.7 copy-start.28
  754.1 5.2 copy-start.15
  759.3 6.2 copy-start.59
  765.6 254.3 %copy-start.42 = (f32[4,1,512]{2,1,0:T(1,128)S(1)}, f32[4,1,512]{2,1,0:T(1,128)}, u32[]{:S(2)}) copy-start(f32[4,1,512]{2,1,0:T(1,128)} %copy-done.41) | copy-start | bytes 24580
  765.6 254.3 %copy-start.50 = (f32[1024]{0:T(1024)S(1)}, f32[1024]{0:T(1024)}, u32[]{:S(2)}) copy-start(f32[1024]{0:T(1024)} %copy-done.49) | copy-start | bytes 12292
  1025.9 22.4 %copy-start.17 = (bf16[8,65536]{1,0:T(8,128)(2,1)S(1)}, bf16[8,65536]{1,0:T(8,128)(2,1)}, u32[]{:S(2)}) copy-start(bf16[8,65536]{1,0:T(8,128)(2,1)} %reshape.785) | copy-start | bytes 3145732
  1041.5 20.5 %copy-start.63 = (u32[32]{0:T(128)S(1)}, u32[32]{0:T(128)}, u32[]{:S(2)}) copy-start(u32[32]{0:T(128)} %constant.135) | copy-start | bytes 388
  1055.1 110.9 %copy-start.52 = (f32[1,4,2,128]{3,1,2,0:T(4,128)S(1)}, f32[1,4,2,128]{3,1,2,0:T(4,128)}, u32[]{:S(2)}) copy-start(f32[1,4,2,128]{3,1,2,0:T(4,128)} %copy-done.51) | copy-start | bytes 12292
  1061.9 146.3 %all-gather.24.cloned.1.call-start = ((), (), s32[]{:S(2)}) async-start(), calls=%async_computation.9 | async-start | bytes 4333056 | tf_op jit(solution)/shard_map/all_gather | solution.py:336
  (20 other events, 34.2 us)
Sparse Core Ops, SparseCore 0:
  9.5 20.8 all-gather.11
  32.0 16.6 all-gather.13
  115.7 155.3 all-reduce.13
  272.5 15.6 all-gather.15
  289.6 16.6 all-gather.17
  307.7 16.6 all-gather.19
  334.6 286.7 all-gather.21
  707.2 12.8 reduce-scatter.1
  728.6 291.3 all-reduce.17
  1062.0 97.8 all-reduce.15
  1166.1 41.9 all-gather.23
